TPU v7x, 1024 devices: a whole 4x8x16 slice. The times are simulated.
1024 devices in a mesh: blk: 128 (over z, y_lo, core), dx: 2 (over y_hi), dy: 4 (over x).
Axes of the slice: x: 4, y: 8 (y_hi: 2, y_lo: 4; y = y_hi * 4 + y_lo), z: 16, core: 2. Of those that a mesh axis runs over, the one named last changes fastest.
Arguments:
- orbitals: bfloat16 [16384, 8, 32, 128], P('blk', 'dx', 'dy'), may hold values from -6 to 6
- coupling: float32 [8, 32, 128], P('dx', 'dy'), may hold values from 0.3 to 3
- pot_grad: float32 [3, 8, 32, 128], P(None, 'dx', 'dy'), may hold values from -6 to 6
Outputs:
- spin_orbit: float32 [3, 5, 16384, 128], P(None, None, ('blk', 'dx', 'dy'))
All inputs are finite; a program needn't handle non-finite values.
Results may differ from a plain program's by a relative error of at most 0.0029.
Values may be sent and summed in bfloat16 or wider, within the bound.
A program may use at most 32 MiB of HBM per device.

v0:
```python
import math

import jax
import jax.numpy as jnp
from jax import lax
from jax.sharding import PartitionSpec as P

HALF = 2


def with_halo(cells, sides, width):
    for axis, dim in sides:
        count = lax.axis_size(axis)
        head = lax.slice_in_dim(cells, 0, width, axis=dim)
        tail = lax.slice_in_dim(cells, cells.shape[dim] - width, cells.shape[dim], axis=dim)
        cells = jnp.concatenate(
            [
                lax.ppermute(tail, axis, [(i, (i + 1) % count) for i in range(count)]),
                cells,
                lax.ppermute(head, axis, [((i + 1) % count, i) for i in range(count)]),
            ],
            axis=dim,
        )
    return cells


def from_behind(block, axis, distance):
    devices = range(lax.axis_size(axis))
    route = [((i - distance) % len(devices), i) for i in devices]
    return lax.ppermute(block, axis, route)


def on_device(orbitals, coupling, pot_grad):
    states, width_x, width_y, width_z = orbitals.shape
    cell_count = width_x * width_y * width_z
    weight_scale = 1.0 / math.sqrt(cell_count * lax.axis_size("dx") * lax.axis_size("dy"))
    coeff_field = coupling[None] * pot_grad
    coeff_one, coeff_two, coeff_three = (coeff_field[0], coeff_field[1], coeff_field[2])
    padded = with_halo(orbitals, (("dx", 1), ("dy", 2)), 1)
    grad_x = 0.5 * (
        padded[:, 2:, 1:-1].astype(jnp.float32) - padded[:, :-2, 1:-1].astype(jnp.float32)
    )
    grad_y = 0.5 * (
        padded[:, 1:-1, 2:].astype(jnp.float32) - padded[:, 1:-1, :-2].astype(jnp.float32)
    )
    field_f32 = orbitals.astype(jnp.float32)
    grad_z = 0.5 * (jnp.roll(field_f32, -1, axis=3) - jnp.roll(field_f32, 1, axis=3))
    cross_one = coeff_two * grad_z - coeff_three * grad_y
    cross_two = coeff_three * grad_x - coeff_one * grad_z
    cross_three = coeff_one * grad_y - coeff_two * grad_x
    cross_field = jnp.stack([cross_one, cross_two, cross_three]).astype(jnp.bfloat16)
    cross_field = cross_field.reshape(3, states, cell_count)
    uppers = []
    current = orbitals
    for step_up in range(HALF):
        current = from_behind(current, "blk", -1)
        uppers.append(current)
    lowers = []
    current = orbitals
    for step_down in range(HALF):
        current = from_behind(current, "blk", 1)
        lowers.append(current)
    panels = lowers[::-1] + [orbitals] + uppers

    def make_tile(panel):
        rows_flat = panel.reshape(states, cell_count)
        return (
            jnp.einsum("kjc,ic->kji", cross_field, rows_flat, preferred_element_type=jnp.float32)
            * weight_scale
        )

    stacked = jnp.stack([make_tile(panel) for panel in panels], 1)
    return lax.psum_scatter(stacked, ("dx", "dy"), scatter_dimension=2, tiled=True)


def solution(mesh):
    in_specs = (P("blk", "dx", "dy", None), P("dx", "dy", None), P(None, "dx", "dy", None))
    out_specs = P(None, None, ("blk", "dx", "dy"), None)
    return jax.shard_map(
        on_device, mesh=mesh, in_specs=in_specs, out_specs=out_specs, check_vma=False
    )
```

profile of v0, /device:TPU:1, one launch (start us, length us, event | category | flops | bytes accessed | tf_op | source)
XLA Modules:
  0.0 220.0 jit_solution(11828130140194268775)
XLA Ops:
  6.5 0.0 copy-start
  6.5 0.0 copy-start.3
  6.5 0.0 copy-start.2
  6.5 0.0 reduce-scatter.2.cloned.1.call-start
  6.5 1.7 copy.4
  8.3 4.6 %collective-permute-start.4 = (bf16[128,4,8,128]{3,0,2,1:T(8,128)(2,1)S(1)}, bf16[128,4,8,128]{3,0,2,1:T(8,128)(2,1)S(1)}, u32[]{:S(2)}, u32[]{:S(2)}) collective-permute-start(bf16[128,4,8,128]{3,0,2,1:T(8,128)(2,1)S(1)} %copy.4), channel_id=1, source_target_pairs={{1016,0},{0,8},{8,16},{16,24},{24,32},{32,40},{40,48},{48,56},{56,... | collective-permute-start | bytes 3145736 | tf_op jit(solution)/shard_map/ppermute | solution.py:30
  12.9 13.4 %collective-permute-start.6 = (bf16[128,4,8,128]{3,0,2,1:T(8,128)(2,1)S(1)}, bf16[128,4,8,128]{3,0,2,1:T(8,128)(2,1)S(1)}, u32[]{:S(2)}, u32[]{:S(2)}) collective-permute-start(bf16[128,4,8,128]{3,0,2,1:T(8,128)(2,1)S(1)} %copy.4), channel_id=1, source_target_pairs={{8,0},{16,8},{24,16},{32,24},{40,32},{48,40},{56,48},{64,56},{72,6... | collective-permute-start | bytes 3145736 | tf_op jit(solution)/shard_map/ppermute | solution.py:30
  26.3 1.9 collective-permute-start
  28.2 7.3 %collective-permute-start.1 = (bf16[128,1,8,128]{3,0,2,1:T(8,128)(2,1)S(1)}, bf16[128,1,8,128]{3,0,2,1:T(8,128)(2,1)S(1)}, u32[]{:S(2)}, u32[]{:S(2)}) collective-permute-start(bf16[128,1,8,128]{3,0,2,1:T(8,128)(2,1)S(1)} %get-tuple-element.17), channel_id=1, source_target_pairs={{4,0},{0,4},{5,1},{1,5},{6,2},{2,6},{7,3},{3,7},{12,8},{8,12},{13,... | collective-permute-start | bytes 786440 | tf_op jit(solution)/shard_map/ppermute | solution.py:20
  35.5 0.0 copy-done.3
  35.5 0.0 copy-done.2
  35.6 18.0 %collective-permute-done = bf16[128,1,8,128]{3,0,2,1:T(8,128)(2,1)S(1)} collective-permute-done((bf16[128,1,8,128]{3,0,2,1:T(8,128)(2,1)S(1)}, bf16[128,1,8,128]{3,0,2,1:T(8,128)(2,1)S(1)}, u32[]{:S(2)}, u32[]{:S(2)}) %collective-permute-start) | collective-permute-done | bytes 262176 | tf_op jit(solution)/shard_map/ppermute | solution.py:18
  53.5 0.0 copy-done
  53.6 0.5 copy_convert_fusion
  54.1 5.0 %collective-permute-done.1 = bf16[128,1,8,128]{3,0,2,1:T(8,128)(2,1)S(1)} collective-permute-done((bf16[128,1,8,128]{3,0,2,1:T(8,128)(2,1)S(1)}, bf16[128,1,8,128]{3,0,2,1:T(8,128)(2,1)S(1)}, u32[]{:S(2)}, u32[]{:S(2)}) %collective-permute-start.1) | collective-permute-done | bytes 262176 | tf_op jit(solution)/shard_map/ppermute | solution.py:20
  59.1 4.4 %collective-permute-start.2 = (bf16[128,6,1,128]{3,0,2,1:T(8,128)(2,1)S(1)}, bf16[128,6,1,128]{3,0,2,1:T(8,128)(2,1)S(1)}, u32[]{:S(2)}, u32[]{:S(2)}) collective-permute-start(bf16[128,6,1,128]{3,0,2,1:T(8,128)(2,1)S(1)} %get-tuple-element.13), channel_id=1, source_target_pairs={{1,0},{2,1},{3,2},{0,3},{5,4},{6,5},{7,6},{4,7},{9,8},{10,9},{11,1... | collective-permute-start | bytes 589832 | tf_op jit(solution)/shard_map/ppermute | solution.py:20
  63.5 1.9 collective-permute-start.3
  65.4 0.7 fusion.28
  66.2 0.0 collective-permute-done.4
  66.2 11.0 %collective-permute-start.5 = (bf16[128,4,8,128]{3,0,2,1:T(8,128)(2,1)S(1)}, bf16[128,4,8,128]{3,0,2,1:T(8,128)(2,1)S(1)}, u32[]{:S(2)}, u32[]{:S(2)}) collective-permute-start(bf16[128,4,8,128]{3,0,2,1:T(8,128)(2,1)S(1)} %collective-permute-done.4), channel_id=1, source_target_pairs={{1016,0},{0,8},{8,16},{16,24},{24,32},{32,40},{40,48},{48,56},{56,... | collective-permute-start | bytes 3145736 | tf_op jit(solution)/shard_map/ppermute | solution.py:30
  77.2 0.7 fusion.27
  77.9 0.0 collective-permute-done.2
  77.9 0.0 collective-permute-done.3
  78.0 2.4 %fusion.15 = (bf16[1,128,4,8,128]{4,1,3,2,0:T(8,128)(2,1)S(1)}, f32[128,4,8,128]{3,0,2,1:T(8,128)S(1)}, bf16[1,128,4,8,128]{4,1,3,2,0:T(8,128)(2,1)S(1)}) fusion(f32[4,8,128]{2,1,0:T(8,128)S(1)} %get-tuple-element.18, f32[4,8,128]{2,1,0:T(8,128)S(1)} %get-tuple-element.20, bf16[128,6,1,128]{3,0,2,1:T(8,128)(2,1)S(1)} %collective-permute-done.2, ...), kind=kLoop, calls=%fused_computation.27 | loop fusion | flops 11010048 | bytes 11976704 | tf_op jit(solution)/shard_map/stack | solution.py:51
  80.4 0.6 fusion.16
  81.0 0.0 collective-permute-done.6
  81.0 1.9 collective-permute-start.7
  82.9 16.4 %collective-permute-done.5 = bf16[128,4,8,128]{3,0,2,1:T(8,128)(2,1)S(1)} collective-permute-done((bf16[128,4,8,128]{3,0,2,1:T(8,128)(2,1)S(1)}, bf16[128,4,8,128]{3,0,2,1:T(8,128)(2,1)S(1)}, u32[]{:S(2)}, u32[]{:S(2)}) %collective-permute-start.5) | collective-permute-done | bytes 1048608 | tf_op jit(solution)/shard_map/ppermute | solution.py:30
  99.3 1.0 fusion.14
  100.3 1.0 fusion.11
  101.2 1.0 fusion.8
  102.2 1.0 fusion.5
  103.2 0.0 collective-permute-done.7
  103.2 1.0 fusion.2
  104.2 0.0 copy-start.1
  104.2 1.0 copy-done.1
  105.2 0.0 reduce-scatter.2.cloned.1.call-update
  105.2 106.4 %reduce-scatter.2.cloned.1.call-done = f32[3,5,16,128]{3,2,0,1:T(8,128)} async-done(((f32[3,5,128,128]{3,2,0,1:T(8,128)}), f32[3,5,16,128]{3,2,0,1:T(8,128)}) %reduce-scatter.2.cloned.1.call-update) | async-done | bytes 122896 | tf_op jit(solution)/shard_map/reduce_scatter | solution.py:73
  211.6 1.6 copy.13
  (6 shorter events, 0.1 us)
Async XLA Ops:
  6.5 47.0 %copy-start = (bf16[128,4,8,128]{3,2,1,0:T(8,128)(2,1)S(1)}, bf16[128,4,8,128]{3,2,1,0:T(8,128)(2,1)}, u32[]{:S(2)}) copy-start(bf16[128,4,8,128]{3,2,1,0:T(8,128)(2,1)} %param.3) | copy-start | bytes 3145732
  6.5 29.0 %copy-start.3 = (f32[4,8,128]{2,1,0:T(8,128)S(1)}, f32[4,8,128]{2,1,0:T(8,128)}, u32[]{:S(2)}) copy-start(f32[4,8,128]{2,1,0:T(8,128)} %param.4) | copy-start | bytes 49156
  6.5 29.0 %copy-start.2 = (f32[3,4,8,128]{3,2,1,0:T(8,128)S(1)}, f32[3,4,8,128]{3,2,1,0:T(8,128)}, u32[]{:S(2)}) copy-start(f32[3,4,8,128]{3,2,1,0:T(8,128)} %param.5) | copy-start | bytes 147460
  6.5 205.1 %reduce-scatter.2.cloned.1.call-start = ((), (), s32[]{:S(2)}) async-start(), calls=%async_computation.1 | async-start | bytes 1105920 | tf_op jit(solution)/shard_map/reduce_scatter | solution.py:73
  8.3 57.9 %collective-permute-start.4 = (bf16[128,4,8,128]{3,0,2,1:T(8,128)(2,1)S(1)}, bf16[128,4,8,128]{3,0,2,1:T(8,128)(2,1)S(1)}, u32[]{:S(2)}, u32[]{:S(2)}) collective-permute-start(bf16[128,4,8,128]{3,0,2,1:T(8,128)(2,1)S(1)} %copy.4), channel_id=1, source_target_pairs={{1016,0},{0,8},{8,16},{16,24},{24,32},{32,40},{40,48},{48,56},{56,... | collective-permute-start | bytes 3145736 | tf_op jit(solution)/shard_map/ppermute | solution.py:30
  12.9 68.1 %collective-permute-start.6 = (bf16[128,4,8,128]{3,0,2,1:T(8,128)(2,1)S(1)}, bf16[128,4,8,128]{3,0,2,1:T(8,128)(2,1)S(1)}, u32[]{:S(2)}, u32[]{:S(2)}) collective-permute-start(bf16[128,4,8,128]{3,0,2,1:T(8,128)(2,1)S(1)} %copy.4), channel_id=1, source_target_pairs={{8,0},{16,8},{24,16},{32,24},{40,32},{48,40},{56,48},{64,56},{72,6... | collective-permute-start | bytes 3145736 | tf_op jit(solution)/shard_map/ppermute | solution.py:30
  26.3 27.2 %collective-permute-start = (bf16[128,1,8,128]{3,0,2,1:T(8,128)(2,1)S(1)}, bf16[128,1,8,128]{3,0,2,1:T(8,128)(2,1)S(1)}, u32[]{:S(2)}, u32[]{:S(2)}) collective-permute-start(bf16[128,1,8,128]{3,0,2,1:T(8,128)(2,1)S(1)} %get-tuple-element.16), channel_id=1, source_target_pairs={{0,4},{4,0},{1,5},{5,1},{2,6},{6,2},{3,7},{7,3},{8,12},{12,8},{9,1... | collective-permute-start | bytes 786440 | tf_op jit(solution)/shard_map/ppermute | solution.py:18
  28.2 30.8 %collective-permute-start.1 = (bf16[128,1,8,128]{3,0,2,1:T(8,128)(2,1)S(1)}, bf16[128,1,8,128]{3,0,2,1:T(8,128)(2,1)S(1)}, u32[]{:S(2)}, u32[]{:S(2)}) collective-permute-start(bf16[128,1,8,128]{3,0,2,1:T(8,128)(2,1)S(1)} %get-tuple-element.17), channel_id=1, source_target_pairs={{4,0},{0,4},{5,1},{1,5},{6,2},{2,6},{7,3},{3,7},{12,8},{8,12},{13,... | collective-permute-start | bytes 786440 | tf_op jit(solution)/shard_map/ppermute | solution.py:20
  59.1 18.8 %collective-permute-start.2 = (bf16[128,6,1,128]{3,0,2,1:T(8,128)(2,1)S(1)}, bf16[128,6,1,128]{3,0,2,1:T(8,128)(2,1)S(1)}, u32[]{:S(2)}, u32[]{:S(2)}) collective-permute-start(bf16[128,6,1,128]{3,0,2,1:T(8,128)(2,1)S(1)} %get-tuple-element.13), channel_id=1, source_target_pairs={{1,0},{2,1},{3,2},{0,3},{5,4},{6,5},{7,6},{4,7},{9,8},{10,9},{11,1... | collective-permute-start | bytes 589832 | tf_op jit(solution)/shard_map/ppermute | solution.py:20
  63.5 14.5 %collective-permute-start.3 = (bf16[128,6,1,128]{3,0,2,1:T(8,128)(2,1)S(1)}, bf16[128,6,1,128]{3,0,2,1:T(8,128)(2,1)S(1)}, u32[]{:S(2)}, u32[]{:S(2)}) collective-permute-start(bf16[128,6,1,128]{3,0,2,1:T(8,128)(2,1)S(1)} %get-tuple-element.12), channel_id=1, source_target_pairs={{0,1},{1,2},{2,3},{3,0},{4,5},{5,6},{6,7},{7,4},{8,9},{9,10},{10,1... | collective-permute-start | bytes 589832 | tf_op jit(solution)/shard_map/ppermute | solution.py:18
  66.2 33.1 %collective-permute-start.5 = (bf16[128,4,8,128]{3,0,2,1:T(8,128)(2,1)S(1)}, bf16[128,4,8,128]{3,0,2,1:T(8,128)(2,1)S(1)}, u32[]{:S(2)}, u32[]{:S(2)}) collective-permute-start(bf16[128,4,8,128]{3,0,2,1:T(8,128)(2,1)S(1)} %collective-permute-done.4), channel_id=1, source_target_pairs={{1016,0},{0,8},{8,16},{16,24},{24,32},{32,40},{40,48},{48,56},{56,... | collective-permute-start | bytes 3145736 | tf_op jit(solution)/shard_map/ppermute | solution.py:30
  81.0 22.2 %collective-permute-start.7 = (bf16[128,4,8,128]{3,0,2,1:T(8,128)(2,1)S(1)}, bf16[128,4,8,128]{3,0,2,1:T(8,128)(2,1)S(1)}, u32[]{:S(2)}, u32[]{:S(2)}) collective-permute-start(bf16[128,4,8,128]{3,0,2,1:T(8,128)(2,1)S(1)} %collective-permute-done.6), channel_id=1, source_target_pairs={{8,0},{16,8},{24,16},{32,24},{40,32},{48,40},{56,48},{64,56},{72,6... | collective-permute-start | bytes 3145736 | tf_op jit(solution)/shard_map/ppermute | solution.py:30
  104.2 1.0 copy-start.1
Sparse Core Ops, SparseCore 0:
  105.3 106.2 reduce-scatter.1
where the time goes:
time: 220 us
  waiting for transfers between devices  146 us (66%)
  starting transfers between devices  46.4 us (21%)
  between operations  13.6 us (6%)
  local copies, waits for them, and re-layouts  5.86 us (3%)
  matrix products  4.88 us (2%)
  other arithmetic  3.52 us (2%)
    reduce_scatter x1, waiting for transfers between devices, on_device(): lax.psum_scatter(stacked, ('dx', 'dy'), scatter_dimension=2, tiled=True)  106 us
    ppermute x4, starting transfers between devices, from_behind(): return lax.ppermute(block, axis, route)  30.9 us
    ppermute x2, waiting for transfers between devices, with_halo(): lax.ppermute(tail, axis, [(i, (i + 1) % count) for i in range(count)])  18 us
    ppermute x4, waiting for transfers between devices, from_behind(): return lax.ppermute(block, axis, route)  16.4 us
    ppermute x2, starting transfers between devices, with_halo(): lax.ppermute(head, axis, [((i + 1) % count, i) for i in range(count)])  11.7 us
    ppermute x2, waiting for transfers between devices, with_halo(): lax.ppermute(head, axis, [((i + 1) % count, i) for i in range(count)])  4.95 us
    dot_general x5, matrix products, make_tile(): jnp.einsum('kjc,ic->kji', cross_field, rows_flat, preferred_element_type=...  4.88 us
  transfers between devices with their start and end apart: 9, of which 4 were waited for; matrix products, arithmetic and copies ran while one was open for 4% of the time, Pallas kernels for 0%

commit v1 on v0

v1 whole, which is shorter than its diff:
```python
import functools
import math

import jax
import jax.numpy as jnp
from jax import lax
from jax.experimental import pallas as pl
from jax.experimental.pallas import tpu as pltpu
from jax.sharding import PartitionSpec as P

MESH = pl.DeviceIdType.MESH
BF16 = jnp.bfloat16
F32 = jnp.float32
NT = (((1,), (1,)), ((), ()))


def wide(value):
    return jnp.concatenate([value[r] for r in range(value.shape[0])], axis=1)


def kernel(
    n_blk, scale,
    psi, coupling, pot_grad, out,
    pad, cf, cfx, cfy, ct, uv, far, acc, stage, from_dy, half, from_dx, from_one, from_two,
    load_sem, xs, xr, ys, yr, cxs, cxr, cys, cyr, chain_s, chain_r, core_s, core_r,
    sum_s, sum_r, home_s, home_r,
):
    b, dx, dy = lax.axis_index("blk"), lax.axis_index("dx"), lax.axis_index("dy")
    core = lax.rem(b, 2)

    def at(block, x, y):
        return (lax.rem(block + n_blk, n_blk), x, lax.rem(y + 4, 4))

    partner = at(b, 1 - dx, dy)
    mate = at(b + 1 - 2 * core, dx, dy)

    def remote(src, dst, send, recv, device):
        return pltpu.make_async_remote_copy(
            src_ref=src, dst_ref=dst, send_sem=send, recv_sem=recv, device_id=device, device_id_type=MESH
        )

    barrier = pltpu.get_barrier_semaphore()
    sources = [partner, mate, at(b + 2, dx, dy)]
    sources += [at(b, dx, dy + o) for o in (1, 2, 3)]
    sources += [at(b - d, x, dy) for d in (1, 2) for x in (0, 1)]
    for device in sources:
        pl.semaphore_signal(barrier, inc=1, device_id=device, device_id_type=MESH)

    own = pad.at[pl.ds(1, 4), pl.ds(1, 8)]
    load = pltpu.make_async_copy(psi, own, load_sem)
    load.start()
    for k in range(3):
        cf[k] = coupling[...] * pot_grad[k]
    load.wait()
    pl.semaphore_wait(barrier, len(sources))

    x_copies = [
        remote(pad.at[4, pl.ds(1, 8)], pad.at[0, pl.ds(1, 8)], xs.at[0], xr.at[0], partner),
        remote(pad.at[1, pl.ds(1, 8)], pad.at[5, pl.ds(1, 8)], xs.at[1], xr.at[1], partner),
        remote(cf.at[:, 3], cfx.at[:, 0], cxs.at[0], cxr.at[0], partner),
        remote(cf.at[:, 0], cfx.at[:, 1], cxs.at[1], cxr.at[1], partner),
    ]
    y_copies = [
        remote(pad.at[pl.ds(1, 4), 8], pad.at[pl.ds(1, 4), 0], ys.at[0], yr.at[0], at(b, dx, dy + 1)),
        remote(pad.at[pl.ds(1, 4), 1], pad.at[pl.ds(1, 4), 9], ys.at[1], yr.at[1], at(b, dx, dy - 1)),
        remote(cf, cfy.at[0], cys.at[0], cyr.at[0], at(b, dx, dy + 1)),
        remote(cf, cfy.at[1], cys.at[1], cyr.at[1], at(b, dx, dy - 1)),
    ]
    for copy in x_copies[2:] + y_copies[2:] + y_copies[:2] + x_copies[:2]:
        copy.start()
    order = (1, 2, 0, 3)
    chain = [
        remote(pad.at[l + 1, pl.ds(1, 8)], far.at[1, l], chain_s.at[l], chain_r.at[l], at(b - 2, dx, dy))
        for l in range(4)
    ]
    hand = [remote(pad.at[l + 1, pl.ds(1, 8)], far.at[0, l], core_s.at[l], core_r.at[l], mate) for l in range(4)]
    pass_on = [remote(far.at[1, l], far.at[0, l], core_s.at[l], core_r.at[l], mate) for l in range(4)]
    for l in order:
        chain[l].start()

    @pl.when(core == 1)
    def _():
        for l in order:
            hand[l].start()

    for copy in x_copies[2:] + y_copies[2:]:
        copy.wait_recv()
    row = lax.broadcasted_iota(jnp.int32, (8, 128), 0)
    for l in range(4):
        here = [cf[k, l] * 0.5 for k in range(3)]
        for k in range(3):
            ct[k, l] = here[k]
        up = [(cf[k, l + 1] if l < 3 else cfx[k, 1]) * 0.5 for k in range(3)]
        down = [(cf[k, l - 1] if l > 0 else cfx[k, 0]) * 0.5 for k in range(3)]
        ct[3, l] = up[1]
        ct[4, l] = up[2]
        ct[5, l] = down[1]
        ct[6, l] = down[2]
        for n, k in ((7, 0), (8, 2)):
            ct[n, l] = jnp.where(row == 7, pltpu.roll(cfy[1, k, l] * 0.5, 7, 0), pltpu.roll(here[k], 7, 0))
            ct[n + 2, l] = jnp.where(row == 0, pltpu.roll(cfy[0, k, l] * 0.5, 1, 0), pltpu.roll(here[k], 1, 0))
        for n, k in ((11, 0), (12, 1)):
            ct[n, l] = pltpu.roll(here[k], 127, 1)
            ct[n + 2, l] = pltpu.roll(here[k], 1, 1)

    rows = 32

    def fields_of(l):
        def one_row(r, carry):
            c = [jnp.broadcast_to(ct[n, l, pl.ds(r, 1), :], (rows, 128)) for n in range(15)]
            c1, c2, c3, c2xp, c3xp, c2xm, c3xm, c1yp, c3yp, c1ym, c3ym, c1zp, c2zp, c1zm, c2zm = c
            for j in range(128 // rows):
                part = pl.ds(j * rows, rows)
                mid = pad[l + 1, r + 1, part, :].astype(F32)
                xp = pad[l + 2, r + 1, part, :].astype(F32)
                xm = pad[l, r + 1, part, :].astype(F32)
                yp = pad[l + 1, r + 2, part, :].astype(F32)
                ym = pad[l + 1, r, part, :].astype(F32)
                zp = pltpu.roll(mid, 127, 1)
                zm = pltpu.roll(mid, 1, 1)
                g1, g2, g3 = xp - xm, yp - ym, zp - zm
                uv[0, l, r, part, :] = (c2 * g3 - c3 * g2).astype(BF16)
                uv[1, l, r, part, :] = (c3 * g1 - c1 * g3).astype(BF16)
                uv[2, l, r, part, :] = (c1 * g2 - c2 * g1).astype(BF16)
                uv[3, l, r, part, :] = ((c3yp * yp - c3ym * ym) - (c2zp * zp - c2zm * zm)).astype(BF16)
                uv[4, l, r, part, :] = ((c1zp * zp - c1zm * zm) - (c3xp * xp - c3xm * xm)).astype(BF16)
                uv[5, l, r, part, :] = ((c2xp * xp - c2xm * xm) - (c1yp * yp - c1ym * ym)).astype(BF16)
            return carry

        lax.fori_loop(0, 8, one_row, 0)

    def left(k, l):
        return wide(uv[k, l])

    def add_own(l, first):
        right = wide(pad[l + 1, pl.ds(1, 8)])
        for k in range(3):
            part = lax.dot_general(left(k, l), right, NT, preferred_element_type=F32)
            acc[k] = part if first else acc[k] + part

    def add_far(l, first):
        q = jnp.concatenate([wide(far[0, l]), wide(far[1, l])], axis=0)
        for k in range(3):
            part = lax.dot_general(left(k, l), q, NT, preferred_element_type=F32)
            for side in range(2):
                piece = part[:, side * 128 : side * 128 + 128]
                t = 3 + 3 * side + k
                acc[t] = piece if first else acc[t] + piece
            part = lax.dot_general(q, left(3 + k, l), NT, preferred_element_type=F32)
            for side in range(2):
                piece = part[side * 128 : side * 128 + 128]
                t = 9 + 3 * side + k
                acc[t] = piece if first else acc[t] + piece

    def send_sums(tiles, group):
        for t in range(tiles.start, tiles.start + tiles.size):
            stage[t] = acc[t].astype(BF16).reshape(2, 4, 16, 128)
        copies = []
        for o in (1, 2, 3):
            to = lax.rem(dy + o, 4)
            copy = remote(
                stage.at[tiles, :, to], from_dy.at[o - 1, tiles],
                sum_s.at[group, o - 1], sum_r.at[group, o - 1], at(b, dx, dy + o),
            )
            copy.start()
            copies.append(copy)
        return copies

    def sums(t, x):
        total = acc[t, pl.ds(pl.multiple_of((x * 4 + dy) * 16, 16), 16), :]
        for o in range(3):
            total = total + from_dy[o, t, x].astype(F32)
        return total

    for copy in y_copies[:2]:
        copy.wait_recv()
    for n, l in enumerate(order):
        if l == 0:
            for copy in x_copies[:2]:
                copy.wait_recv()
        fields_of(l)
        add_own(l, n == 0)
    first_sums = send_sums(pl.ds(0, 3), 0)

    for n, l in enumerate(order):
        chain[l].wait_recv()

        @pl.when(core == 0)
        def _(l=l):
            pass_on[l].start()

        hand[l].wait_recv()
        add_far(l, n == 0)
    last_sums = send_sums(pl.ds(3, 12), 1)

    other = 1 - dx
    for copy in first_sums + last_sums:
        copy.wait_recv()
    for t in range(9):
        half[t] = sums(t, other)
    home = [remote(half.at[pl.ds(0, 9)], from_dx, home_s.at[0], home_r.at[0], partner)]
    home[0].start()
    for x in range(2):
        for k in range(3):
            half[9 + 6 * x + k] = sums(9 + k, x)
            half[12 + 6 * x + k] = sums(12 + k, x)
        one = remote(
            half.at[pl.ds(9 + 6 * x, 3)], from_one.at[dx], home_s.at[1 + x], home_r.at[1 + dx], at(b + 1, x, dy)
        )
        two = remote(
            half.at[pl.ds(12 + 6 * x, 3)], from_two.at[dx], home_s.at[3 + x], home_r.at[3 + dx], at(b + 2, x, dy)
        )
        one.start()
        two.start()
        home += [one, two]

    home[0].wait_recv()
    for k in range(3):
        for t in range(3):
            out[k, 2 + t] = (sums(3 * t + k, dx) + from_dx[3 * t + k]) * scale
    for x in range(2):
        arrived = remote(half.at[pl.ds(9, 3)], from_one.at[x], home_s.at[1 + x], home_r.at[1 + x], partner)
        arrived.wait_recv()
        arrived = remote(half.at[pl.ds(12, 3)], from_two.at[x], home_s.at[3 + x], home_r.at[3 + x], partner)
        arrived.wait_recv()
    for k in range(3):
        out[k, 1] = (from_one[0, k] + from_one[1, k]) * scale
        out[k, 0] = (from_two[0, k] + from_two[1, k]) * scale

    for copy in x_copies + y_copies + chain + first_sums + last_sums + home:
        copy.wait_send()
    for l in range(4):
        hand[l].wait_send()


def on_device(n_blk, scale, orbitals, coupling, pot_grad):
    psi = orbitals.transpose(1, 2, 0, 3)
    dma = pltpu.SemaphoreType.DMA
    vmem = pl.BlockSpec(memory_space=pltpu.VMEM)
    return pl.pallas_call(
        functools.partial(kernel, n_blk, scale),
        out_shape=jax.ShapeDtypeStruct((3, 5, 16, 128), F32),
        in_specs=[pl.BlockSpec(memory_space=pl.ANY), vmem, vmem],
        out_specs=vmem,
        scratch_shapes=[
            pltpu.VMEM((6, 10, 128, 128), BF16),
            pltpu.VMEM((3, 4, 8, 128), F32),
            pltpu.VMEM((3, 2, 8, 128), F32),
            pltpu.VMEM((2, 3, 4, 8, 128), F32),
            pltpu.VMEM((15, 4, 8, 128), F32),
            pltpu.VMEM((6, 4, 8, 128, 128), BF16),
            pltpu.VMEM((2, 4, 8, 128, 128), BF16),
            pltpu.VMEM((15, 128, 128), F32),
            pltpu.VMEM((15, 2, 4, 16, 128), BF16),
            pltpu.VMEM((3, 15, 2, 16, 128), BF16),
            pltpu.VMEM((21, 16, 128), F32),
            pltpu.VMEM((9, 16, 128), F32),
            pltpu.VMEM((2, 3, 16, 128), F32),
            pltpu.VMEM((2, 3, 16, 128), F32),
            dma, dma((2,)), dma((2,)), dma((2,)), dma((2,)), dma((2,)), dma((2,)), dma((2,)), dma((2,)),
            dma((4,)), dma((4,)), dma((4,)), dma((4,)),
            dma((2, 3)), dma((2, 3)), dma((5,)), dma((5,)),
        ],
        compiler_params=pltpu.CompilerParams(
            collective_id=0, has_side_effects=True, vmem_limit_bytes=56 * 1024 * 1024
        ),
    )(psi, coupling, pot_grad)


def solution(mesh):
    cells = 8 * 32 * 128
    in_specs = (P("blk", "dx", "dy", None), P("dx", "dy", None), P(None, "dx", "dy", None))
    out_specs = P(None, None, ("blk", "dx", "dy"), None)
    return jax.shard_map(
        functools.partial(on_device, mesh.shape["blk"], 1.0 / math.sqrt(cells)),
        mesh=mesh, in_specs=in_specs, out_specs=out_specs, check_vma=False,
    )
```

time: 220 us -> 85.6 us (0.39)
  the two profiles are of different devices: /device:TPU:1 before, /device:TPU:961 now
where the time goes in v1:
time: 85.6 us; the launch traced here: 84.7 us
  Pallas kernels  80.5 us (94%)
  local copies, waits for them, and re-layouts  4.18 us (5%)
    pallas_call x1, Pallas kernels, on_device(): pl.pallas_call(functools.partial(kernel, n_blk, scale), out_shape=jax.Sha...  80.5 us
    unnamed x2, local copies, waits for them, and re-layouts  4.18 us

profile of v1, /device:TPU:961, one launch (start us, length us, event | category | flops | bytes accessed | tf_op | source)
XLA Modules:
  0.0 84.7 jit_solution(10614847210550778620)
XLA Ops:
  0.0 2.6 %copy.6 = bf16[128,4,8,128]{3,0,2,1:T(8,128)(2,1)} copy(bf16[128,4,8,128]{3,2,1,0:T(8,128)(2,1)} %param.3) | data formatting | bytes 2097152 | tf_op args[0]
  2.6 80.5 %shard_map.37 = f32[3,5,16,128]{3,2,1,0:T(8,128)} custom-call(bf16[4,8,128,128]{3,2,1,0:T(8,128)(2,1)} %bitcast.3, f32[4,8,128]{2,1,0:T(8,128)} %coupling.1, f32[3,4,8,128]{3,2,1,0:T(8,128)} %pot_grad.1), custom_call_target="tpu_custom_call" | custom-call | tf_op jit(solution)/shard_map/pallas_call | solution.py:240
  83.2 1.6 %copy.8 = f32[3,5,16,128]{3,2,1,0:T(8,128)} copy(f32[3,5,16,128]{3,2,1,0:T(8,128)} %shard_map.37) | data formatting | bytes 245760

commit v2 on v1

v2 whole, which is shorter than its diff:
```python
import functools
import math

import jax
import jax.numpy as jnp
from jax import lax
from jax.experimental import pallas as pl
from jax.experimental.pallas import tpu as pltpu
from jax.sharding import PartitionSpec as P

MESH = pl.DeviceIdType.MESH
BF16 = jnp.bfloat16
F32 = jnp.float32
NT = (((1,), (1,)), ((), ()))


def wide(value):
    return jnp.concatenate([value[r] for r in range(value.shape[0])], axis=1)


def kernel(
    n_blk, scale,
    psi, coupling, pot_grad, out,
    flat, pad, cf, cfx, cfy, ct, uv, far, lent, acc, stage, from_dy, half, from_dx, from_one, from_two,
    xs, xr, ys, yr, cxs, cxr, cys, cyr, hand_s, lend_s, lend_r, chain_s, pass_s, far_r,
    sum_s, sum_r, home_s, home_r, late,
):
    b, dx, dy = lax.axis_index("blk"), lax.axis_index("dx"), lax.axis_index("dy")
    core = lax.rem(b, 2)

    def at(block, x, y):
        return (lax.rem(block + n_blk, n_blk), x, lax.rem(y + 4, 4))

    def is_root(device):
        return (device[0] == 0) & (device[1] == 0) & (device[2] == 0)

    partner = at(b, 1 - dx, dy)
    mate = at(b + 1 - 2 * core, dx, dy)
    above, below = at(b, dx, dy + 1), at(b, dx, dy - 1)

    def remote(src, dst, send, recv, device):
        return pltpu.make_async_remote_copy(
            src_ref=src, dst_ref=dst, send_sem=send, recv_sem=recv, device_id=device, device_id_type=MESH
        )

    friends = [partner] + [at(b, dx, dy + o) for o in (1, 2, 3)]
    friends += [at(b + d, x, dy) for d in (-2, -1, 1, 2) for x in (0, 1)]
    root = is_root((b, dx, dy))
    near = jnp.int32(0)
    for device in friends:
        near = near + is_root(device).astype(jnp.int32)
    barrier = pltpu.get_barrier_semaphore()

    @pl.when(jnp.logical_not(root))
    def _():
        for device in friends:
            pl.semaphore_signal(barrier, inc=1, device_id=device, device_id_type=MESH)

    for k in range(3):
        cf[k] = coupling[...] * pot_grad[k]

    for j in range(8):
        flat[pl.ds(j * 512, 512), :] = psi[pl.ds(j * 16, 16)].astype(F32).reshape(512, 128)
    for l in (0, 3, 1, 2):

        def turn(r, carry, l=l):
            pad[l + 1, r + 1] = flat[pl.ds(l * 8 + r, 128, stride=32), :].astype(BF16)
            return carry

        lax.fori_loop(0, 8, turn, 0)
    pl.semaphore_wait(barrier, len(friends) - near)

    @pl.when(root)
    def _():
        for device in friends:
            pl.semaphore_signal(late, inc=1, device_id=device, device_id_type=MESH)

    ends = pl.ds(1, 8)
    layers = pl.ds(1, 4)
    x_copies = [
        remote(pad.at[4, ends], pad.at[0, ends], xs.at[0], xr.at[0], partner),
        remote(pad.at[1, ends], pad.at[5, ends], xs.at[1], xr.at[1], partner),
    ]
    cx_copies = [
        remote(cf.at[:, 3], cfx.at[:, 0], cxs.at[0], cxr.at[0], partner),
        remote(cf.at[:, 0], cfx.at[:, 1], cxs.at[1], cxr.at[1], partner),
    ]
    y_copies = [
        remote(pad.at[layers, 8], pad.at[layers, 0], ys.at[0], yr.at[0], above),
        remote(pad.at[layers, 1], pad.at[layers, 9], ys.at[1], yr.at[1], below),
    ]
    cy_copies = [
        remote(cf, cfy.at[0], cys.at[0], cyr.at[0], above),
        remote(cf, cfy.at[1], cys.at[1], cyr.at[1], below),
    ]
    hand = [remote(pad.at[l + 1, ends], far.at[0, l], hand_s.at[l], far_r.at[0, l], mate) for l in range(4)]
    lend = [remote(pad.at[3 * i + 1, ends], lent.at[i], lend_s.at[i], lend_r.at[i], mate) for i in range(2)]

    def start_first(when):
        groups = [
            (partner, cx_copies + x_copies),
            (above, [cy_copies[0], y_copies[0]]),
            (below, [cy_copies[1], y_copies[1]]),
        ]
        for device, copies in groups:

            @pl.when(when(device))
            def _(copies=copies):
                for copy in copies:
                    copy.start()

        @pl.when(when(mate) & (core == 1))
        def _():
            for l in (1, 2, 0, 3):
                hand[l].start()

        @pl.when(when(mate) & (core == 0))
        def _():
            for copy in lend:
                copy.start()

    start_first(lambda device: jnp.logical_not(is_root(device)))

    row = lax.broadcasted_iota(jnp.int32, (8, 128), 0)

    def coefficients(l):
        here = [cf[k, l] * 0.5 for k in range(3)]
        for k in range(3):
            ct[k, l] = here[k]
        up = [(cf[k, l + 1] if l < 3 else cfx[k, 1]) * 0.5 for k in range(3)]
        down = [(cf[k, l - 1] if l > 0 else cfx[k, 0]) * 0.5 for k in range(3)]
        ct[3, l] = up[1]
        ct[4, l] = up[2]
        ct[5, l] = down[1]
        ct[6, l] = down[2]
        for n, k in ((7, 0), (8, 2)):
            ct[n, l] = jnp.where(row == 7, pltpu.roll(cfy[1, k, l] * 0.5, 7, 0), pltpu.roll(here[k], 7, 0))
            ct[n + 2, l] = jnp.where(row == 0, pltpu.roll(cfy[0, k, l] * 0.5, 1, 0), pltpu.roll(here[k], 1, 0))
        for n, k in ((11, 0), (12, 1)):
            ct[n, l] = pltpu.roll(here[k], 127, 1)
            ct[n + 2, l] = pltpu.roll(here[k], 1, 1)

    rows = 32

    def fields_of(l):
        coefficients(l)

        def one_row(r, carry):
            c = [jnp.broadcast_to(ct[n, l, pl.ds(r, 1), :], (rows, 128)) for n in range(15)]
            c1, c2, c3, c2xp, c3xp, c2xm, c3xm, c1yp, c3yp, c1ym, c3ym, c1zp, c2zp, c1zm, c2zm = c
            for j in range(128 // rows):
                part = pl.ds(j * rows, rows)
                mid = pad[l + 1, r + 1, part, :].astype(F32)
                xp = pad[l + 2, r + 1, part, :].astype(F32)
                xm = pad[l, r + 1, part, :].astype(F32)
                yp = pad[l + 1, r + 2, part, :].astype(F32)
                ym = pad[l + 1, r, part, :].astype(F32)
                zp = pltpu.roll(mid, 127, 1)
                zm = pltpu.roll(mid, 1, 1)
                g1, g2, g3 = xp - xm, yp - ym, zp - zm
                uv[0, l, r, part, :] = (c2 * g3 - c3 * g2).astype(BF16)
                uv[1, l, r, part, :] = (c3 * g1 - c1 * g3).astype(BF16)
                uv[2, l, r, part, :] = (c1 * g2 - c2 * g1).astype(BF16)
                uv[3, l, r, part, :] = ((c3yp * yp - c3ym * ym) - (c2zp * zp - c2zm * zm)).astype(BF16)
                uv[4, l, r, part, :] = ((c1zp * zp - c1zm * zm) - (c3xp * xp - c3xm * xm)).astype(BF16)
                uv[5, l, r, part, :] = ((c2xp * xp - c2xm * xm) - (c1yp * yp - c1ym * ym)).astype(BF16)
            return carry

        lax.fori_loop(0, 8, one_row, 0)

    def add(t, part, first):
        acc[t] = part if first else acc[t] + part

    def three(k, l):
        return jnp.concatenate([wide(uv[k + i, l]) for i in range(3)], axis=0)

    def add_own(l, first):
        part = lax.dot_general(three(0, l), wide(pad[l + 1, ends]), NT, preferred_element_type=F32)
        for k in range(3):
            add(k, part[k * 128 : k * 128 + 128], first)

    def add_far(side, l, first):
        q = wide(far[side, l])
        t = 3 + 6 * side
        part = lax.dot_general(three(0, l), q, NT, preferred_element_type=F32)
        for k in range(3):
            add(t + k, part[k * 128 : k * 128 + 128], first)
        part = lax.dot_general(q, three(3, l), NT, preferred_element_type=F32)
        for k in range(3):
            add(t + 3 + k, part[:, k * 128 : k * 128 + 128], first)

    def send_sums(group, first, count):
        for t in range(first, first + count):
            stage[t] = acc[t].astype(BF16).reshape(2, 4, 16, 128)
        tiles = pl.ds(first, count)
        copies = []
        for o in (2, 1, 3):
            copy = remote(
                stage.at[tiles, :, lax.rem(dy + o, 4)], from_dy.at[o - 1, tiles],
                sum_s.at[group, o - 1], sum_r.at[group, o - 1], at(b, dx, dy + o),
            )
            copy.start()
            copies.append(copy)
        return copies

    def sums(t, x):
        total = acc[t, pl.ds(pl.multiple_of((x * 4 + dy) * 16, 16), 16), :]
        for o in range(3):
            total = total + from_dy[o, t, x].astype(F32)
        return total

    other = 1 - dx
    home = []

    def send_home(copy):
        copy.start()
        home.append(copy)

    def to_partner(group, first):
        for k in range(3):
            half[3 * group + k] = sums(first + k, other)
        send_home(
            remote(
                half.at[pl.ds(3 * group, 3)], from_dx.at[group], home_s.at[group], home_r.at[group], partner
            )
        )

    def to_panel(side, first, landing):
        for x in (0, 1):
            for k in range(3):
                half[9 + 6 * side + 3 * x + k] = sums(first + k, x)
            send_home(
                remote(
                    half.at[pl.ds(9 + 6 * side + 3 * x, 3)], landing.at[dx],
                    home_s.at[3 + 2 * side + x], home_r.at[3 + 2 * side + dx], at(b + side + 1, x, dy),
                )
            )

    def arrived(copies):
        for copy in copies:
            copy.wait_recv()

    arrived(cy_copies + y_copies)
    fields_of(1)
    fields_of(2)

    @pl.when(near == 1)
    def _():
        pl.semaphore_wait(late, 1)
        start_first(is_root)

    even_down = [remote(pad.at[l + 1, ends], far.at[1, l], chain_s.at[l - 1], far_r.at[1, l], at(b - 2, dx, dy)) for l in (1, 2)]
    even_down += [remote(far.at[0, l], far.at[1, l], chain_s.at[l + 1], far_r.at[1, l], at(b - 1, dx, dy)) for l in (1, 2)]
    odd_down = [remote(lent.at[i], far.at[0, 3 * i], chain_s.at[i], far_r.at[0, 3 * i], at(b - 2, dx, dy)) for i in (0, 1)]
    odd_down += [remote(pad.at[3 * i + 1, ends], far.at[1, 3 * i], chain_s.at[i + 2], far_r.at[1, 3 * i], at(b - 2, dx, dy)) for i in (0, 1)]

    @pl.when(core == 0)
    def _():
        even_down[0].start()
        even_down[1].start()
        hand[1].wait_recv()
        even_down[2].start()
        hand[2].wait_recv()
        even_down[3].start()

    @pl.when(core == 1)
    def _():
        for i in (0, 1):
            lend[i].wait_recv()
            odd_down[i].start()
        for i in (2, 3):
            odd_down[i].start()

    add_own(1, True)
    add_own(2, False)
    arrived(cx_copies + x_copies)
    for l in (0, 3):
        fields_of(l)
        add_own(l, False)
    first_sums = send_sums(0, 0, 3)

    places = [1 - core, 2 + core, core, 3 - core]

    def take(side, n):
        l = places[n]
        dst = far.at[1 - side, l]
        pass_on = remote(far.at[side, l], dst, pass_s.at[n % 2], far_r.at[1 - side, l], mate)
        slot = remote(far.at[side, l], far.at[side, l], pass_s.at[n % 2], far_r.at[side, l], mate)
        if side == 0:
            if n < 2:

                @pl.when(core == 1)
                def _():
                    slot.wait_recv()
                    pass_on.start()

            else:
                slot.wait_recv()
        else:
            slot.wait_recv()
            if n < 2:

                @pl.when(core == 0)
                def _():
                    pass_on.start()

        add_far(side, l, n == 0)
        return pass_on

    passed = []
    for n in range(4):
        passed.append(take(0, n))
    one_sums = send_sums(1, 3, 6)
    arrived(first_sums)
    to_partner(0, 0)
    for n in range(3):
        take(1, n)
    arrived(one_sums)
    to_partner(1, 3)
    to_panel(0, 6, from_one)
    take(1, 3)
    two_sums = send_sums(2, 9, 6)

    def waited(side, x, landing):
        copy = remote(
            half.at[pl.ds(9, 3)], landing.at[x], home_s.at[3 + 2 * side + x], home_r.at[3 + 2 * side + x], partner
        )
        copy.wait_recv()

    def own_rows(group, first):
        home[group if group == 0 else (1 if group == 1 else 4)].wait_recv()
        for k in range(3):
            out[k, 2 + group] = (sums(first + k, dx) + from_dx[group, k]) * scale

    own_rows(0, 0)
    own_rows(1, 3)
    for x in (0, 1):
        waited(0, x, from_one)
    for k in range(3):
        out[k, 1] = (from_one[0, k] + from_one[1, k]) * scale
    arrived(two_sums)
    to_partner(2, 9)
    to_panel(1, 12, from_two)
    own_rows(2, 9)
    for x in (0, 1):
        waited(1, x, from_two)
    for k in range(3):
        out[k, 0] = (from_two[0, k] + from_two[1, k]) * scale

    for copy in x_copies + cx_copies + y_copies + cy_copies + first_sums + one_sums + two_sums + home + even_down:
        copy.wait_send()
    for n in (0, 1):
        passed[n].wait_send()

    @pl.when(core == 0)
    def _():
        for copy in lend:
            copy.wait_send()

    @pl.when(core == 1)
    def _():
        for copy in hand:
            copy.wait_send()


def on_device(n_blk, scale, orbitals, coupling, pot_grad):
    dma = pltpu.SemaphoreType.DMA
    vmem = pl.BlockSpec(memory_space=pltpu.VMEM)
    return pl.pallas_call(
        functools.partial(kernel, n_blk, scale),
        out_shape=jax.ShapeDtypeStruct((3, 5, 16, 128), F32),
        in_specs=[vmem, vmem, vmem],
        out_specs=vmem,
        scratch_shapes=[
            pltpu.VMEM((4096, 128), F32),
            pltpu.VMEM((6, 10, 128, 128), BF16),
            pltpu.VMEM((3, 4, 8, 128), F32),
            pltpu.VMEM((3, 2, 8, 128), F32),
            pltpu.VMEM((2, 3, 4, 8, 128), F32),
            pltpu.VMEM((15, 4, 8, 128), F32),
            pltpu.VMEM((6, 4, 8, 128, 128), BF16),
            pltpu.VMEM((2, 4, 8, 128, 128), BF16),
            pltpu.VMEM((2, 8, 128, 128), BF16),
            pltpu.VMEM((15, 128, 128), F32),
            pltpu.VMEM((15, 2, 4, 16, 128), BF16),
            pltpu.VMEM((3, 15, 2, 16, 128), BF16),
            pltpu.VMEM((21, 16, 128), F32),
            pltpu.VMEM((3, 3, 16, 128), F32),
            pltpu.VMEM((2, 3, 16, 128), F32),
            pltpu.VMEM((2, 3, 16, 128), F32),
            dma((2,)), dma((2,)), dma((2,)), dma((2,)), dma((2,)), dma((2,)), dma((2,)), dma((2,)),
            dma((4,)), dma((2,)), dma((2,)), dma((4,)), dma((2,)), dma((2, 4)),
            dma((3, 3)), dma((3, 3)), dma((7,)), dma((7,)), pltpu.SemaphoreType.REGULAR,
        ],
        compiler_params=pltpu.CompilerParams(
            collective_id=0, has_side_effects=True, vmem_limit_bytes=32 * 1024 * 1024
        ),
    )(orbitals, coupling, pot_grad)


def solution(mesh):
    cells = 8 * 32 * 128
    in_specs = (P("blk", "dx", "dy", None), P("dx", "dy", None), P(None, "dx", "dy", None))
    out_specs = P(None, None, ("blk", "dx", "dy"), None)
    return jax.shard_map(
        functools.partial(on_device, mesh.shape["blk"], 1.0 / math.sqrt(cells)),
        mesh=mesh, in_specs=in_specs, out_specs=out_specs, check_vma=False,
    )
```

time: 85.6 us -> 85.2 us (level)
    unnamed x2 -> x7, local copies, waits for them, and re-layouts: 4.18 us -> 3.39 us
where the time goes in v2:
time: 85.2 us; the launch traced here: 83.8 us
  Pallas kernels  80.4 us (94%)
  local copies, waits for them, and re-layouts  3.39 us (4%)
    pallas_call x1, Pallas kernels, on_device(): pl.pallas_call(functools.partial(kernel, n_blk, scale), out_shape=jax.Sha...  80.4 us
    unnamed x7, local copies, waits for them, and re-layouts  3.39 us

profile of v2, /device:TPU:961, one launch (start us, length us, event | category | flops | bytes accessed | tf_op | source)
XLA Modules:
  0.0 83.8 jit_solution(11061611331338505237)
XLA Ops:
  0.0 0.0 copy-start
  0.0 1.2 %copy-done = bf16[128,4,8,128]{3,2,1,0:T(8,128)(2,1)S(1)} copy-done((bf16[128,4,8,128]{3,2,1,0:T(8,128)(2,1)S(1)}, bf16[128,4,8,128]{3,2,1,0:T(8,128)(2,1)}, u32[]{:S(2)}) %copy-start) | copy-done | bytes 1048600
  1.2 0.0 copy-start.1
  1.2 0.8 copy-done.1
  2.0 0.0 copy-start.2
  2.0 0.7 copy-done.2
  2.7 80.4 %shard_map.37 = f32[3,5,16,128]{3,2,1,0:T(8,128)S(1)} custom-call(bf16[128,4,8,128]{3,2,1,0:T(8,128)(2,1)S(1)} %copy-done, f32[4,8,128]{2,1,0:T(8,128)S(1)} %copy-done.2, f32[3,4,8,128]{3,2,1,0:T(8,128)S(1)} %copy-done.1), custom_call_target="tpu_custom_call" | custom-call | tf_op jit(solution)/shard_map/pallas_call | solution.py:369
  83.1 0.7 copy.5
Async XLA Ops:
  0.0 1.2 %copy-start = (bf16[128,4,8,128]{3,2,1,0:T(8,128)(2,1)S(1)}, bf16[128,4,8,128]{3,2,1,0:T(8,128)(2,1)}, u32[]{:S(2)}) copy-start(bf16[128,4,8,128]{3,2,1,0:T(8,128)(2,1)} %psi.1) | copy-start | bytes 3145732
  1.2 0.8 copy-start.1
  2.0 0.7 copy-start.2

commit v3 on v2

--- a/solution.py
+++ b/solution.py
@@ -20,9 +20,9 @@
 
 def kernel(
     n_blk, scale,
-    psi, coupling, pot_grad, out,
-    flat, pad, cf, cfx, cfy, ct, uv, far, lent, acc, stage, from_dy, half, from_dx, from_one, from_two,
-    xs, xr, ys, yr, cxs, cxr, cys, cyr, hand_s, lend_s, lend_r, chain_s, pass_s, far_r,
+    psi_in, coupling_in, pot_grad_in, out,
+    psi, coupling, pot_grad, flat, pad, cf, cfx, cfy, ct, uv, far, lent, acc, stage, from_dy, half, from_dx, from_one, from_two,
+    load_sem, xs, xr, ys, yr, cxs, cxr, cys, cyr, hand_s, lend_s, lend_r, chain_s, pass_s, far_r,
     sum_s, sum_r, home_s, home_r, late,
 ):
     b, dx, dy = lax.axis_index("blk"), lax.axis_index("dx"), lax.axis_index("dy")
@@ -42,6 +42,13 @@
         return pltpu.make_async_remote_copy(
             src_ref=src, dst_ref=dst, send_sem=send, recv_sem=recv, device_id=device, device_id_type=MESH
         )
+
+    loads = [
+        pltpu.make_async_copy(src, dst, load_sem.at[i])
+        for i, (src, dst) in enumerate(((psi_in, psi), (coupling_in, coupling), (pot_grad_in, pot_grad)))
+    ]
+    for load in loads:
+        load.start()
 
     friends = [partner] + [at(b, dx, dy + o) for o in (1, 2, 3)]
     friends += [at(b + d, x, dy) for d in (-2, -1, 1, 2) for x in (0, 1)]
@@ -56,15 +63,17 @@
         for device in friends:
             pl.semaphore_signal(barrier, inc=1, device_id=device, device_id_type=MESH)
 
+    for load in loads:
+        load.wait()
     for k in range(3):
         cf[k] = coupling[...] * pot_grad[k]
 
     for j in range(8):
         flat[pl.ds(j * 512, 512), :] = psi[pl.ds(j * 16, 16)].astype(F32).reshape(512, 128)
-    for l in (0, 3, 1, 2):
+    for l in range(4):
 
         def turn(r, carry, l=l):
-            pad[l + 1, r + 1] = flat[pl.ds(l * 8 + r, 128, stride=32), :].astype(BF16)
+            pad[l, r + 1] = flat[pl.ds(l * 8 + r, 128, stride=32), :].astype(BF16)
             return carry
 
         lax.fori_loop(0, 8, turn, 0)
@@ -76,15 +85,9 @@
             pl.semaphore_signal(late, inc=1, device_id=device, device_id_type=MESH)
 
     ends = pl.ds(1, 8)
-    layers = pl.ds(1, 4)
-    x_copies = [
-        remote(pad.at[4, ends], pad.at[0, ends], xs.at[0], xr.at[0], partner),
-        remote(pad.at[1, ends], pad.at[5, ends], xs.at[1], xr.at[1], partner),
-    ]
-    cx_copies = [
-        remote(cf.at[:, 3], cfx.at[:, 0], cxs.at[0], cxr.at[0], partner),
-        remote(cf.at[:, 0], cfx.at[:, 1], cxs.at[1], cxr.at[1], partner),
-    ]
+    layers = pl.ds(0, 4)
+    x_copies = [remote(pad.at[0, ends], pad.at[4, ends], xs, xr, partner)]
+    cx_copies = [remote(cf.at[:, 0], cfx, cxs, cxr, partner)]
     y_copies = [
         remote(pad.at[layers, 8], pad.at[layers, 0], ys.at[0], yr.at[0], above),
         remote(pad.at[layers, 1], pad.at[layers, 9], ys.at[1], yr.at[1], below),
@@ -93,8 +96,18 @@
         remote(cf, cfy.at[0], cys.at[0], cyr.at[0], above),
         remote(cf, cfy.at[1], cys.at[1], cyr.at[1], below),
     ]
-    hand = [remote(pad.at[l + 1, ends], far.at[0, l], hand_s.at[l], far_r.at[0, l], mate) for l in range(4)]
-    lend = [remote(pad.at[3 * i + 1, ends], lent.at[i], lend_s.at[i], lend_r.at[i], mate) for i in range(2)]
+    hand = [remote(pad.at[l, ends], far.at[0, l], hand_s.at[l], far_r.at[0, l], mate) for l in range(5)]
+    lend = [remote(pad.at[3 * i, ends], lent.at[i], lend_s.at[i], lend_r.at[i], mate) for i in range(2)]
+
+    chip_before = at(b - 2, dx, dy)
+
+    def down(src, side, l, n, device):
+        return remote(src, far.at[side, l], chain_s.at[n], far_r.at[side, l], device)
+
+    even_down = [down(pad.at[l, ends], 1, l, n, chip_before) for n, l in enumerate((1, 2, 4))]
+    even_down += [down(far.at[0, l], 1, l, 2 + l, at(b - 1, dx, dy)) for l in (1, 2)]
+    odd_down = [down(lent.at[i], 0, 3 * i, i, chip_before) for i in (0, 1)]
+    odd_down += [down(pad.at[l, ends], 1, l, n, chip_before) for n, l in ((2, 0), (3, 3), (4, 4))]
 
     def start_first(when):
         groups = [
@@ -119,6 +132,11 @@
             for copy in lend:
                 copy.start()
 
+        @pl.when(when(chip_before) & (core == 0))
+        def _():
+            even_down[0].start()
+            even_down[1].start()
+
     start_first(lambda device: jnp.logical_not(is_root(device)))
 
     row = lax.broadcasted_iota(jnp.int32, (8, 128), 0)
@@ -127,12 +145,10 @@
         here = [cf[k, l] * 0.5 for k in range(3)]
         for k in range(3):
             ct[k, l] = here[k]
-        up = [(cf[k, l + 1] if l < 3 else cfx[k, 1]) * 0.5 for k in range(3)]
-        down = [(cf[k, l - 1] if l > 0 else cfx[k, 0]) * 0.5 for k in range(3)]
-        ct[3, l] = up[1]
-        ct[4, l] = up[2]
-        ct[5, l] = down[1]
-        ct[6, l] = down[2]
+        for n, k in ((3, 1), (4, 2)):
+            ct[n, l] = (cf[k, l + 1] if l < 3 else cfx[k]) * 0.5
+            if l > 0:
+                ct[n + 2, l] = cf[k, l - 1] * 0.5
         for n, k in ((7, 0), (8, 2)):
             ct[n, l] = jnp.where(row == 7, pltpu.roll(cfy[1, k, l] * 0.5, 7, 0), pltpu.roll(here[k], 7, 0))
             ct[n + 2, l] = jnp.where(row == 0, pltpu.roll(cfy[0, k, l] * 0.5, 1, 0), pltpu.roll(here[k], 1, 0))
@@ -146,24 +162,43 @@
         coefficients(l)
 
         def one_row(r, carry):
-            c = [jnp.broadcast_to(ct[n, l, pl.ds(r, 1), :], (rows, 128)) for n in range(15)]
+            c = [None if l == 0 and n in (5, 6) else jnp.broadcast_to(ct[n, l, pl.ds(r, 1), :], (rows, 128)) for n in range(15)]
             c1, c2, c3, c2xp, c3xp, c2xm, c3xm, c1yp, c3yp, c1ym, c3ym, c1zp, c2zp, c1zm, c2zm = c
             for j in range(128 // rows):
                 part = pl.ds(j * rows, rows)
-                mid = pad[l + 1, r + 1, part, :].astype(F32)
-                xp = pad[l + 2, r + 1, part, :].astype(F32)
-                xm = pad[l, r + 1, part, :].astype(F32)
-                yp = pad[l + 1, r + 2, part, :].astype(F32)
-                ym = pad[l + 1, r, part, :].astype(F32)
+                mid = pad[l, r + 1, part, :].astype(F32)
+                xp = pad[l + 1, r + 1, part, :].astype(F32)
+                yp = pad[l, r + 2, part, :].astype(F32)
+                ym = pad[l, r, part, :].astype(F32)
                 zp = pltpu.roll(mid, 127, 1)
                 zm = pltpu.roll(mid, 1, 1)
-                g1, g2, g3 = xp - xm, yp - ym, zp - zm
+                g1, g2, g3 = xp, yp - ym, zp - zm
+                c2x, c3x = c2xp * xp, c3xp * xp
+                if l > 0:
+                    xm = pad[l - 1, r + 1, part, :].astype(F32)
+                    g1, c2x, c3x = g1 - xm, c2x - c2xm * xm, c3x - c3xm * xm
                 uv[0, l, r, part, :] = (c2 * g3 - c3 * g2).astype(BF16)
                 uv[1, l, r, part, :] = (c3 * g1 - c1 * g3).astype(BF16)
                 uv[2, l, r, part, :] = (c1 * g2 - c2 * g1).astype(BF16)
                 uv[3, l, r, part, :] = ((c3yp * yp - c3ym * ym) - (c2zp * zp - c2zm * zm)).astype(BF16)
-                uv[4, l, r, part, :] = ((c1zp * zp - c1zm * zm) - (c3xp * xp - c3xm * xm)).astype(BF16)
-                uv[5, l, r, part, :] = ((c2xp * xp - c2xm * xm) - (c1yp * yp - c1ym * ym)).astype(BF16)
+                uv[4, l, r, part, :] = ((c1zp * zp - c1zm * zm) - c3x).astype(BF16)
+                uv[5, l, r, part, :] = (c2x - (c1yp * yp - c1ym * ym)).astype(BF16)
+            return carry
+
+        lax.fori_loop(0, 8, one_row, 0)
+
+    def fields_at_the_end():
+        for n, k in ((0, 1), (1, 2)):
+            ct[n, 4] = cfx[k] * 0.5
+
+        def one_row(r, carry):
+            c2, c3 = [jnp.broadcast_to(ct[n, 4, pl.ds(r, 1), :], (128, 128)) for n in (0, 1)]
+            c2xm, c3xm = [jnp.broadcast_to(ct[n, 3, pl.ds(r, 1), :], (128, 128)) for n in (1, 2)]
+            xm = pad[3, r + 1].astype(F32)
+            uv[1, 4, r] = (-(c3 * xm)).astype(BF16)
+            uv[2, 4, r] = (c2 * xm).astype(BF16)
+            uv[4, 4, r] = (c3xm * xm).astype(BF16)
+            uv[5, 4, r] = (-(c2xm * xm)).astype(BF16)
             return carry
 
         lax.fori_loop(0, 8, one_row, 0)
@@ -171,23 +206,22 @@
     def add(t, part, first):
         acc[t] = part if first else acc[t] + part
 
-    def three(k, l):
-        return jnp.concatenate([wide(uv[k + i, l]) for i in range(3)], axis=0)
-
-    def add_own(l, first):
-        part = lax.dot_general(three(0, l), wide(pad[l + 1, ends]), NT, preferred_element_type=F32)
-        for k in range(3):
-            add(k, part[k * 128 : k * 128 + 128], first)
-
-    def add_far(side, l, first):
+    def fields(k, l, end):
+        return jnp.concatenate([wide(uv[k + i, l]) for i in range(1 if end else 0, 3)], axis=0)
+
+    def add_own(l, first, end=False):
+        part = lax.dot_general(fields(0, l, end), wide(pad[l, ends]), NT, preferred_element_type=F32)
+        for i, k in enumerate((1, 2) if end else (0, 1, 2)):
+            add(k, part[i * 128 : i * 128 + 128], first)
+
+    def add_far(side, l, first, end=False):
         q = wide(far[side, l])
         t = 3 + 6 * side
-        part = lax.dot_general(three(0, l), q, NT, preferred_element_type=F32)
-        for k in range(3):
-            add(t + k, part[k * 128 : k * 128 + 128], first)
-        part = lax.dot_general(q, three(3, l), NT, preferred_element_type=F32)
-        for k in range(3):
-            add(t + 3 + k, part[:, k * 128 : k * 128 + 128], first)
+        part = lax.dot_general(fields(0, l, end), q, NT, preferred_element_type=F32)
+        back = lax.dot_general(q, fields(3, l, end), NT, preferred_element_type=F32)
+        for i, k in enumerate((1, 2) if end else (0, 1, 2)):
+            add(t + k, part[i * 128 : i * 128 + 128], first)
+            add(t + 3 + k, back[:, i * 128 : i * 128 + 128], first)
 
     def send_sums(group, first, count):
         for t in range(first, first + count):
@@ -241,51 +275,54 @@
             copy.wait_recv()
 
     arrived(cy_copies + y_copies)
-    fields_of(1)
-    fields_of(2)
-
-    @pl.when(near == 1)
-    def _():
-        pl.semaphore_wait(late, 1)
-        start_first(is_root)
-
-    even_down = [remote(pad.at[l + 1, ends], far.at[1, l], chain_s.at[l - 1], far_r.at[1, l], at(b - 2, dx, dy)) for l in (1, 2)]
-    even_down += [remote(far.at[0, l], far.at[1, l], chain_s.at[l + 1], far_r.at[1, l], at(b - 1, dx, dy)) for l in (1, 2)]
-    odd_down = [remote(lent.at[i], far.at[0, 3 * i], chain_s.at[i], far_r.at[0, 3 * i], at(b - 2, dx, dy)) for i in (0, 1)]
-    odd_down += [remote(pad.at[3 * i + 1, ends], far.at[1, 3 * i], chain_s.at[i + 2], far_r.at[1, 3 * i], at(b - 2, dx, dy)) for i in (0, 1)]
-
-    @pl.when(core == 0)
-    def _():
-        even_down[0].start()
-        even_down[1].start()
-        hand[1].wait_recv()
-        even_down[2].start()
-        hand[2].wait_recv()
-        even_down[3].start()
+    fields_of(0)
 
     @pl.when(core == 1)
     def _():
         for i in (0, 1):
             lend[i].wait_recv()
             odd_down[i].start()
-        for i in (2, 3):
-            odd_down[i].start()
-
-    add_own(1, True)
-    add_own(2, False)
+        odd_down[2].start()
+        odd_down[3].start()
+
+    fields_of(1)
+    fields_of(2)
+
+    @pl.when(near == 1)
+    def _():
+        pl.semaphore_wait(late, 1)
+        start_first(is_root)
+
+    for l in range(3):
+        add_own(l, l == 0)
     arrived(cx_copies + x_copies)
-    for l in (0, 3):
-        fields_of(l)
-        add_own(l, False)
+
+    @pl.when(core == 0)
+    def _():
+        even_down[2].start()
+        for l in (1, 2):
+            hand[l].wait_recv()
+            even_down[2 + l].start()
+
+    @pl.when(core == 1)
+    def _():
+        odd_down[4].start()
+        hand[4].start()
+
+    fields_of(3)
+    fields_at_the_end()
+    add_own(3, False)
+    add_own(4, False, True)
     first_sums = send_sums(0, 0, 3)
 
-    places = [1 - core, 2 + core, core, 3 - core]
+    places = [1 - core, 2 + core, core, 3 - core, 4]
 
     def take(side, n):
         l = places[n]
-        dst = far.at[1 - side, l]
-        pass_on = remote(far.at[side, l], dst, pass_s.at[n % 2], far_r.at[1 - side, l], mate)
-        slot = remote(far.at[side, l], far.at[side, l], pass_s.at[n % 2], far_r.at[side, l], mate)
+        pass_on = remote(
+            far.at[side, l], far.at[1 - side, l], pass_s.at[min(n, 2) if n != 4 else 2], far_r.at[1 - side, l], mate
+        )
+        slot = remote(far.at[side, l], far.at[side, l], pass_s.at[0], far_r.at[side, l], mate)
         if side == 0:
             if n < 2:
 
@@ -298,27 +335,27 @@
                 slot.wait_recv()
         else:
             slot.wait_recv()
-            if n < 2:
+            if n in (0, 1, 4):
 
                 @pl.when(core == 0)
                 def _():
                     pass_on.start()
 
-        add_far(side, l, n == 0)
+        add_far(side, l, n == 0, n == 4)
         return pass_on
 
     passed = []
-    for n in range(4):
+    for n in range(5):
         passed.append(take(0, n))
     one_sums = send_sums(1, 3, 6)
     arrived(first_sums)
     to_partner(0, 0)
-    for n in range(3):
+    for n in range(4):
         take(1, n)
     arrived(one_sums)
     to_partner(1, 3)
     to_panel(0, 6, from_one)
-    take(1, 3)
+    take(1, 4)
     two_sums = send_sums(2, 9, 6)
 
     def waited(side, x, landing):
@@ -354,6 +391,7 @@
 
     @pl.when(core == 0)
     def _():
+        passed[4].wait_send()
         for copy in lend:
             copy.wait_send()
 
@@ -369,17 +407,20 @@
     return pl.pallas_call(
         functools.partial(kernel, n_blk, scale),
         out_shape=jax.ShapeDtypeStruct((3, 5, 16, 128), F32),
-        in_specs=[vmem, vmem, vmem],
+        in_specs=[pl.BlockSpec(memory_space=pltpu.HBM)] * 3,
         out_specs=vmem,
         scratch_shapes=[
+            pltpu.VMEM((128, 4, 8, 128), BF16),
+            pltpu.VMEM((4, 8, 128), F32),
+            pltpu.VMEM((3, 4, 8, 128), F32),
             pltpu.VMEM((4096, 128), F32),
-            pltpu.VMEM((6, 10, 128, 128), BF16),
+            pltpu.VMEM((5, 10, 128, 128), BF16),
             pltpu.VMEM((3, 4, 8, 128), F32),
-            pltpu.VMEM((3, 2, 8, 128), F32),
+            pltpu.VMEM((3, 8, 128), F32),
             pltpu.VMEM((2, 3, 4, 8, 128), F32),
-            pltpu.VMEM((15, 4, 8, 128), F32),
-            pltpu.VMEM((6, 4, 8, 128, 128), BF16),
-            pltpu.VMEM((2, 4, 8, 128, 128), BF16),
+            pltpu.VMEM((15, 5, 8, 128), F32),
+            pltpu.VMEM((6, 5, 8, 128, 128), BF16),
+            pltpu.VMEM((2, 5, 8, 128, 128), BF16),
             pltpu.VMEM((2, 8, 128, 128), BF16),
             pltpu.VMEM((15, 128, 128), F32),
             pltpu.VMEM((15, 2, 4, 16, 128), BF16),
@@ -388,12 +429,12 @@
             pltpu.VMEM((3, 3, 16, 128), F32),
             pltpu.VMEM((2, 3, 16, 128), F32),
             pltpu.VMEM((2, 3, 16, 128), F32),
-            dma((2,)), dma((2,)), dma((2,)), dma((2,)), dma((2,)), dma((2,)), dma((2,)), dma((2,)),
-            dma((4,)), dma((2,)), dma((2,)), dma((4,)), dma((2,)), dma((2, 4)),
+            dma((3,)), dma, dma, dma((2,)), dma((2,)), dma, dma, dma((2,)), dma((2,)),
+            dma((5,)), dma((2,)), dma((2,)), dma((5,)), dma((3,)), dma((2, 5)),
             dma((3, 3)), dma((3, 3)), dma((7,)), dma((7,)), pltpu.SemaphoreType.REGULAR,
         ],
         compiler_params=pltpu.CompilerParams(
-            collective_id=0, has_side_effects=True, vmem_limit_bytes=32 * 1024 * 1024
+            collective_id=0, has_side_effects=True, vmem_limit_bytes=67043328 - 128 * 1024
         ),
     )(orbitals, coupling, pot_grad)
 

time: 85.2 us -> 78.6 us (0.923); the launches traced: 83.8 us -> 78.5 us
  Pallas kernels: 80.4 us -> 76.9 us
  local copies, waits for them, and re-layouts: 3.39 us -> 1.56 us
    pallas_call x1, Pallas kernels: 80.4 us -> 76.9 us  [on_device(): pl.pallas_call(functools.partial(kernel, n_blk, scale), out_shape=jax.Sha...]
    unnamed x7 -> x1, local copies, waits for them, and re-layouts: 3.39 us -> 1.56 us
where the time goes in v3:
time: 78.6 us; the launch traced here: 78.5 us
  Pallas kernels  76.9 us (98%)
  local copies, waits for them, and re-layouts  1.56 us (2%)
    pallas_call x1, Pallas kernels, on_device(): pl.pallas_call(functools.partial(kernel, n_blk, scale), out_shape=jax.Sha...  76.9 us

profile of v3, /device:TPU:961, one launch (start us, length us, event | category | flops | bytes accessed | tf_op | source)
XLA Modules:
  0.0 78.5 jit_solution(12754896802711161734)
XLA Ops:
  0.0 76.9 %shard_map.37 = f32[3,5,16,128]{3,2,1,0:T(8,128)} custom-call(bf16[128,4,8,128]{3,2,1,0:T(8,128)(2,1)} %psi_in.1, f32[4,8,128]{2,1,0:T(8,128)} %coupling_in.1, f32[3,4,8,128]{3,2,1,0:T(8,128)} %pot_grad_in.1), custom_call_target="tpu_custom_call" | custom-call | tf_op jit(solution)/shard_map/pallas_call | solution.py:407
  76.9 1.6 %copy.5 = f32[3,5,16,128]{3,2,1,0:T(8,128)} copy(f32[3,5,16,128]{3,2,1,0:T(8,128)} %shard_map.37) | data formatting | bytes 245760

commit v4 on v3

--- a/solution.py
+++ b/solution.py
@@ -214,14 +214,15 @@
         for i, k in enumerate((1, 2) if end else (0, 1, 2)):
             add(k, part[i * 128 : i * 128 + 128], first)
 
+    def add_back(side, l, first, end=False):
+        back = lax.dot_general(wide(far[side, l]), fields(3, l, end), NT, preferred_element_type=F32)
+        for i, k in enumerate((1, 2) if end else (0, 1, 2)):
+            add(6 + 6 * side + k, back[:, i * 128 : i * 128 + 128], first)
+
     def add_far(side, l, first, end=False):
-        q = wide(far[side, l])
-        t = 3 + 6 * side
-        part = lax.dot_general(fields(0, l, end), q, NT, preferred_element_type=F32)
-        back = lax.dot_general(q, fields(3, l, end), NT, preferred_element_type=F32)
+        part = lax.dot_general(fields(0, l, end), wide(far[side, l]), NT, preferred_element_type=F32)
         for i, k in enumerate((1, 2) if end else (0, 1, 2)):
-            add(t + k, part[i * 128 : i * 128 + 128], first)
-            add(t + 3 + k, back[:, i * 128 : i * 128 + 128], first)
+            add(3 + 6 * side + k, part[i * 128 : i * 128 + 128], first)
 
     def send_sums(group, first, count):
         for t in range(first, first + count):
@@ -341,7 +342,9 @@
                 def _():
                     pass_on.start()
 
-        add_far(side, l, n == 0, n == 4)
+        add_back(side, l, n == 0, n == 4)
+        if side == 0 or n < 4:
+            add_far(side, l, n == 0, n == 4)
         return pass_on
 
     passed = []
@@ -356,7 +359,13 @@
     to_partner(1, 3)
     to_panel(0, 6, from_one)
     take(1, 4)
-    two_sums = send_sums(2, 9, 6)
+    back_sums = send_sums(2, 12, 3)
+    add_far(1, 4, False, True)
+    two_sums = send_sums(3, 9, 3)
+    arrived(back_sums)
+    to_panel(1, 12, from_two)
+    arrived(two_sums)
+    to_partner(2, 9)
 
     def waited(side, x, landing):
         copy = remote(
@@ -365,7 +374,7 @@
         copy.wait_recv()
 
     def own_rows(group, first):
-        home[group if group == 0 else (1 if group == 1 else 4)].wait_recv()
+        home[(0, 1, 6)[group]].wait_recv()
         for k in range(3):
             out[k, 2 + group] = (sums(first + k, dx) + from_dx[group, k]) * scale
 
@@ -375,16 +384,13 @@
         waited(0, x, from_one)
     for k in range(3):
         out[k, 1] = (from_one[0, k] + from_one[1, k]) * scale
-    arrived(two_sums)
-    to_partner(2, 9)
-    to_panel(1, 12, from_two)
     own_rows(2, 9)
     for x in (0, 1):
         waited(1, x, from_two)
     for k in range(3):
         out[k, 0] = (from_two[0, k] + from_two[1, k]) * scale
 
-    for copy in x_copies + cx_copies + y_copies + cy_copies + first_sums + one_sums + two_sums + home + even_down:
+    for copy in x_copies + cx_copies + y_copies + cy_copies + first_sums + one_sums + back_sums + two_sums + home + even_down:
         copy.wait_send()
     for n in (0, 1):
         passed[n].wait_send()
@@ -431,7 +437,7 @@
             pltpu.VMEM((2, 3, 16, 128), F32),
             dma((3,)), dma, dma, dma((2,)), dma((2,)), dma, dma, dma((2,)), dma((2,)),
             dma((5,)), dma((2,)), dma((2,)), dma((5,)), dma((3,)), dma((2, 5)),
-            dma((3, 3)), dma((3, 3)), dma((7,)), dma((7,)), pltpu.SemaphoreType.REGULAR,
+            dma((4, 3)), dma((4, 3)), dma((7,)), dma((7,)), pltpu.SemaphoreType.REGULAR,
         ],
         compiler_params=pltpu.CompilerParams(
             collective_id=0, has_side_effects=True, vmem_limit_bytes=67043328 - 128 * 1024

time: 78.6 us -> 78.7 us (level)
  no operation moved by 1% of the time
where the time goes in v4:
time: 78.7 us; the launch traced here: 78.5 us
  Pallas kernels  76.9 us (98%)
  local copies, waits for them, and re-layouts  1.56 us (2%)
    pallas_call x1, Pallas kernels, on_device(): pl.pallas_call(functools.partial(kernel, n_blk, scale), out_shape=jax.Sha...  76.9 us

profile of v4, /device:TPU:961, one launch (start us, length us, event | category | flops | bytes accessed | tf_op | source)
XLA Modules:
  0.0 78.5 jit_solution(37525962788147701)
XLA Ops:
  0.0 76.9 %shard_map.37 = f32[3,5,16,128]{3,2,1,0:T(8,128)} custom-call(bf16[128,4,8,128]{3,2,1,0:T(8,128)(2,1)} %psi_in.1, f32[4,8,128]{2,1,0:T(8,128)} %coupling_in.1, f32[3,4,8,128]{3,2,1,0:T(8,128)} %pot_grad_in.1), custom_call_target="tpu_custom_call" | custom-call | tf_op jit(solution)/shard_map/pallas_call | solution.py:413
  76.9 1.6 %copy.5 = f32[3,5,16,128]{3,2,1,0:T(8,128)} copy(f32[3,5,16,128]{3,2,1,0:T(8,128)} %shard_map.37) | data formatting | bytes 245760

commit v5 on v4

--- a/solution.py
+++ b/solution.py
@@ -294,6 +294,12 @@
         pl.semaphore_wait(late, 1)
         start_first(is_root)
 
+    @pl.when(core == 0)
+    def _():
+        for l in (1, 2):
+            hand[l].wait_recv()
+            even_down[2 + l].start()
+
     for l in range(3):
         add_own(l, l == 0)
     arrived(cx_copies + x_copies)
@@ -301,9 +307,6 @@
     @pl.when(core == 0)
     def _():
         even_down[2].start()
-        for l in (1, 2):
-            hand[l].wait_recv()
-            even_down[2 + l].start()
 
     @pl.when(core == 1)
     def _():

time: 78.7 us -> 78.4 us (level)
  no operation moved by 1% of the time
where the time goes in v5:
time: 78.4 us; the launch traced here: 78.2 us
  Pallas kernels  76.6 us (98%)
  local copies, waits for them, and re-layouts  1.56 us (2%)
    pallas_call x1, Pallas kernels, on_device(): pl.pallas_call(functools.partial(kernel, n_blk, scale), out_shape=jax.Sha...  76.6 us

profile of v5, /device:TPU:961, one launch (start us, length us, event | category | flops | bytes accessed | tf_op | source)
XLA Modules:
  0.0 78.2 jit_solution(591890572414005570)
XLA Ops:
  0.0 76.6 %shard_map.37 = f32[3,5,16,128]{3,2,1,0:T(8,128)} custom-call(bf16[128,4,8,128]{3,2,1,0:T(8,128)(2,1)} %psi_in.1, f32[4,8,128]{2,1,0:T(8,128)} %coupling_in.1, f32[3,4,8,128]{3,2,1,0:T(8,128)} %pot_grad_in.1), custom_call_target="tpu_custom_call" | custom-call | tf_op jit(solution)/shard_map/pallas_call | solution.py:416
  76.6 1.6 %copy.5 = f32[3,5,16,128]{3,2,1,0:T(8,128)} copy(f32[3,5,16,128]{3,2,1,0:T(8,128)} %shard_map.37) | data formatting | bytes 245760
